TPU v7x, 512 devices: a whole 4x4x16 slice. The times are simulated.
512 devices in a mesh: row: 16 (over y, x), col: 32 (over z, core).
Axes of the slice: x: 4, y: 4, z: 16, core: 2. Of those that a mesh axis runs over, the one named last changes fastest.
Arguments:
- root_inverse: bfloat16 [4096, 4096], P('row', 'col'), may hold values from -16 to 16
- factor: bfloat16 [4096, 4, 4096], P('row', None, 'col'), may hold values from -0.59765625 to 0.59765625
- inverse_diag: bfloat16 [4096, 4, 4096], P('row', None, 'col'), may hold values from -6 to 6
- structure: int32 [4, 32], replicated, may hold values 0 or 1
Outputs:
- ainv_rk: bfloat16 [4096, 4, 4096], P('row', None, 'col')
- ainv_kk: bfloat16 [4096, 4, 4096], P('row', None, 'col')
All inputs are finite; a program needn't handle non-finite values.
Results may differ from a plain program's by a relative error of at most 0.014.
Values may be sent and summed in bfloat16 or wider, within the bound.
No kernel may reach another device: no remote copies, remote signals or barrier semaphores. Data moves between devices by JAX's collectives and lax.ppermute only.
A program may use at most 64 MiB of HBM per device.

v0:
```python
import jax
import jax.numpy as jnp
from jax import lax
from jax.sharding import PartitionSpec as P

BLK = 128


def body(root_inverse, factor, inverse_diag, structure):
    local_rows = factor.shape[0]
    offset = lax.axis_index("row") * local_rows
    row_mask = jnp.repeat(structure, BLK, axis=1)
    local_mask = lax.dynamic_slice_in_dim(row_mask, offset, local_rows, 1).T.astype(factor.dtype)
    masked = factor * local_mask[:, :, None]
    root_rows = lax.all_gather(root_inverse, "col", axis=1, tiled=True)
    product = jnp.einsum(
        "ik,knj->inj",
        root_rows,
        lax.all_gather(masked, "row", axis=0, tiled=True),
        preferred_element_type=jnp.float32,
    )
    ainv_rk = (-product).astype(jnp.bfloat16)
    inverse_rows = lax.all_gather(ainv_rk, "col", axis=2, tiled=True)
    running = lax.psum_scatter(
        jnp.einsum("kni,knj->inj", inverse_rows, masked, preferred_element_type=jnp.float32).astype(
            jnp.bfloat16
        ),
        "row",
        scatter_dimension=0,
        tiled=True,
    ).astype(jnp.float32)
    ainv_kk = (inverse_diag.astype(jnp.float32) - running).astype(jnp.bfloat16)
    return (ainv_rk, ainv_kk)


def solution(mesh):
    return jax.shard_map(
        body,
        mesh=mesh,
        in_specs=(P("row", "col"), P("row", None, "col"), P("row", None, "col"), P()),
        out_specs=(P("row", None, "col"), P("row", None, "col")),
        check_vma=False,
    )
```

profile of v0, /device:TPU:32, one launch (start us, length us, event | category | flops | bytes accessed | tf_op | source)
XLA Modules:
  0.0 349.0 jit_solution(17044077061663513549)
XLA Ops:
  7.2 0.0 copy-start
  7.2 0.0 all-gather.6.cloned.1.call-start
  7.2 0.7 all-gather.6.cloned.1.call-update
  7.9 0.0 all-gather.4.cloned.1.call-start
  8.0 0.0 copy-done
  8.0 0.1 broadcast_bitcast_fusion
  8.0 0.1 copy.14
  8.1 1.1 copy.6
  9.2 0.7 broadcast_multiply_fusion
  10.0 0.0 all-gather.4.cloned.1.call-update
  10.0 0.0 copy-start.1
  10.0 0.0 all-gather.8.cloned.1.call-start
  10.0 76.9 %all-gather.6.cloned.1.call-done = bf16[256,4096]{1,0:T(8,128)(2,1)} async-done(((bf16[256,128]{1,0:T(8,128)(2,1)}), bf16[256,4096]{1,0:T(8,128)(2,1)}) %all-gather.6.cloned.1.call-update) | async-done | bytes 2097168 | tf_op jit(solution)/shard_map/all_gather | solution.py:15
  86.9 71.7 %all-gather.4.cloned.1.call-done = bf16[4096,4,128]{0,2,1:T(8,128)(2,1)} async-done(((bf16[256,4,128]{0,2,1:T(8,128)(2,1)}), bf16[4096,4,128]{0,2,1:T(8,128)(2,1)}) %all-gather.4.cloned.1.call-update) | async-done | bytes 4194320 | tf_op jit(solution)/shard_map/all_gather | solution.py:19
  158.6 4.9 %fusion.9 = bf16[256,4,128]{0,2,1:T(8,128)(2,1)} fusion(bf16[4096,4,128]{0,2,1:T(8,128)(2,1)} %all-gather.4.cloned.1.call-done, bf16[256,4096]{1,0:T(8,128)(2,1)} %all-gather.6.cloned.1.call-done), kind=kOutput, calls=%fused_computation.6 | convolution fusion | flops 1074003968 | bytes 6553600 | tf_op jit(solution)/shard_map/ik,knj->inj/dot_general | solution.py:16
  163.5 0.0 all-gather.8.cloned.1.call-update
  163.5 0.0 reduce-scatter.2.cloned.1.call-start
  163.5 78.3 %all-gather.8.cloned.1.call-done = bf16[256,4,4096]{0,2,1:T(8,128)(2,1)} async-done(((bf16[256,4,128]{0,2,1:T(8,128)(2,1)}), bf16[256,4,4096]{0,2,1:T(8,128)(2,1)}) %all-gather.8.cloned.1.call-update) | async-done | bytes 8388624 | tf_op jit(solution)/shard_map/all_gather | solution.py:23
  241.9 0.0 copy-done.1
  241.9 8.2 %fusion = bf16[4096,4,128]{0,2,1:T(8,128)(2,1)} fusion(bf16[256,4,128]{0,2,1:T(8,128)(2,1)S(1)} %copy-done.1, bf16[256,4,4096]{0,2,1:T(8,128)(2,1)} %all-gather.8.cloned.1.call-done), kind=kOutput, calls=%fused_computation.1 | convolution fusion | flops 1075838976 | bytes 12845056 | tf_op jit(solution)/shard_map/kni,knj->inj/dot_general | solution.py:25
  250.1 0.0 copy-start.3
  250.1 0.0 copy-start.2
  250.1 0.0 reduce-scatter.2.cloned.1.call-update
  250.1 0.9 copy-done.3
  251.0 0.2 copy.7
  251.2 0.0 copy-done.2
  251.2 0.9 copy.9
  252.1 88.5 %reduce-scatter.2.cloned.1.call-done = bf16[256,4,128]{0,2,1:T(8,128)(2,1)} async-done(((bf16[4096,4,128]{0,2,1:T(8,128)(2,1)}), bf16[256,4,128]{0,2,1:T(8,128)(2,1)}) %reduce-scatter.2.cloned.1.call-update) | async-done | bytes 262160 | tf_op jit(solution)/shard_map/reduce_scatter | solution.py:24
  340.6 1.0 subtract_convert_fusion
  341.6 0.9 copy.10
  (1 shorter events, 0.0 us)
Async XLA Ops:
  7.2 0.8 copy-start
  7.2 79.7 %all-gather.6.cloned.1.call-start = ((), (), s32[]{:S(2)}) async-start(), calls=%async_computation.2 | async-start | bytes 2162688 | tf_op jit(solution)/shard_map/all_gather | solution.py:15
  7.9 150.7 %all-gather.4.cloned.1.call-start = ((), (), s32[]{:S(2)}) async-start(), calls=%async_computation.1 | async-start | bytes 4456448 | tf_op jit(solution)/shard_map/all_gather | solution.py:19
  10.0 231.9 %copy-start.1 = (bf16[256,4,128]{0,2,1:T(8,128)(2,1)S(1)}, bf16[256,4,128]{0,2,1:T(8,128)(2,1)}, u32[]{:S(2)}) copy-start(bf16[256,4,128]{0,2,1:T(8,128)(2,1)} %broadcast_multiply_fusion) | copy-start | bytes 786436
  10.0 231.9 %all-gather.8.cloned.1.call-start = ((), (), s32[]{:S(2)}) async-start(), calls=%async_computation.3 | async-start | bytes 8650752 | tf_op jit(solution)/shard_map/all_gather | solution.py:23
  163.5 177.1 %reduce-scatter.2.cloned.1.call-start = ((), (), s32[]{:S(2)}) async-start(), calls=%async_computation.4 | async-start | bytes 4456448 | tf_op jit(solution)/shard_map/reduce_scatter | solution.py:24
  250.1 0.9 copy-start.3
  250.1 1.1 copy-start.2
Sparse Core Ops, SparseCore 0:
  10.0 76.8 all-gather.5
  90.5 68.0 all-gather.3
  163.6 78.2 all-gather.7
  250.2 90.3 reduce-scatter.1
where the time goes:
time: 349 us
  waiting for transfers between devices  316 us (91%)
  between operations  13.8 us (4%)
  matrix products  13 us (4%)
  local copies, waits for them, and re-layouts  4.08 us (1%)
    reduce_scatter x1, waiting for transfers between devices, body(): lax.psum_scatter(jnp.einsum('kni,knj->inj', inverse_rows, masked, preferr...  88.5 us
    all_gather x1, waiting for transfers between devices, body(): inverse_rows = lax.all_gather(ainv_rk, 'col', axis=2, tiled=True)  78.3 us
    all_gather x1, waiting for transfers between devices, body(): root_rows = lax.all_gather(root_inverse, 'col', axis=1, tiled=True)  76.9 us
    all_gather x1, waiting for transfers between devices, body(): lax.all_gather(masked, 'row', axis=0, tiled=True)  71.7 us
    dot_general x1, matrix products, body(): jnp.einsum('kni,knj->inj', inverse_rows, masked, preferred_element_type=j...  8.19 us
  transfers between devices with their start and end apart: 4, of which 4 were waited for; matrix products, arithmetic and copies ran while one was open for 1% of the time, Pallas kernels for 0%

commit v1 on v0

--- a/solution.py
+++ b/solution.py
@@ -12,7 +12,9 @@
     row_mask = jnp.repeat(structure, BLK, axis=1)
     local_mask = lax.dynamic_slice_in_dim(row_mask, offset, local_rows, 1).T.astype(factor.dtype)
     masked = factor * local_mask[:, :, None]
-    root_rows = lax.all_gather(root_inverse, "col", axis=1, tiled=True)
+    root_rows = jnp.concatenate(
+        lax.all_to_all(jnp.stack([root_inverse] * lax.axis_size("col")), "col", 0, 0), axis=1
+    )
     product = jnp.einsum(
         "ik,knj->inj",
         root_rows,

time: 349 us -> 314 us (0.90)
  waiting for transfers between devices: 316 us -> 259 us
  starting transfers between devices: 0.16 us -> 15.5 us
  local copies, waits for them, and re-layouts: 4.08 us -> 11.4 us
    all_to_all x0 -> x1, waiting for transfers between devices: none -> 98.9 us  [body(): lax.all_to_all(jnp.stack([root_inverse] * lax.axis_size('col')), 'col', 0...]
    all_gather x1 -> x0, waiting for transfers between devices: 76.9 us -> none  [body(): root_rows = lax.all_gather(root_inverse, 'col', axis=1, tiled=True)]
    all_gather x1, waiting for transfers between devices: 71.7 us -> 0.02 us  [body(): lax.all_gather(masked, 'row', axis=0, tiled=True)]
    all_to_all x0 -> x1, starting transfers between devices: none -> 15.4 us  [body(): lax.all_to_all(jnp.stack([root_inverse] * lax.axis_size('col')), 'col', 0...]
    all_gather x1, waiting for transfers between devices: 78.3 us -> 71.3 us  [body(): inverse_rows = lax.all_gather(ainv_rk, 'col', axis=2, tiled=True)]
    reshape x0 -> x2, local copies, waits for them, and re-layouts: none -> 5.51 us  [body(): jnp.concatenate(lax.all_to_all(jnp.stack([root_inverse] * lax.axis_size('...]
  transfers between devices with their start and end apart: 4 -> 4, of which waited for: 4 -> 3; matrix products, arithmetic and copies ran while one was open for 1% -> 2% of each run, Pallas kernels for 0% -> 0%
where the time goes in v1:
time: 314 us
  waiting for transfers between devices  259 us (82%)
  starting transfers between devices  15.5 us (5%)
  between operations  13.9 us (4%)
  matrix products  12.4 us (4%)
  local copies, waits for them, and re-layouts  11.4 us (4%)
    all_to_all x1, waiting for transfers between devices, body(): lax.all_to_all(jnp.stack([root_inverse] * lax.axis_size('col')), 'col', 0...  98.9 us
    reduce_scatter x1, waiting for transfers between devices, body(): lax.psum_scatter(jnp.einsum('kni,knj->inj', inverse_rows, masked, preferr...  88.5 us
    all_gather x1, waiting for transfers between devices, body(): inverse_rows = lax.all_gather(ainv_rk, 'col', axis=2, tiled=True)  71.3 us
    all_to_all x1, starting transfers between devices, body(): lax.all_to_all(jnp.stack([root_inverse] * lax.axis_size('col')), 'col', 0...  15.4 us
    dot_general x1, matrix products, body(): jnp.einsum('kni,knj->inj', inverse_rows, masked, preferred_element_type=j...  8.18 us
  transfers between devices with their start and end apart: 4, of which 3 were waited for; matrix products, arithmetic and copies ran while one was open for 2% of the time, Pallas kernels for 0%

profile of v1, /device:TPU:32, one launch (start us, length us, event | category | flops | bytes accessed | tf_op | source)
XLA Modules:
  0.0 313.6 jit_solution(11268897736941292034)
XLA Ops:
  7.2 0.0 copy-start
  7.2 0.0 copy-start.3
  7.2 2.7 stack.2
  9.9 15.4 %all-to-all-start = ((bf16[32,256,128]{2,1,0:T(8,128)(2,1)}), bf16[32,256,128]{2,1,0:T(8,128)(2,1)S(1)}, u32[]{:S(2)}, u32[]{:S(2)}) async-start(bf16[32,256,128]{2,1,0:T(8,128)(2,1)} %stack.2), calls=%async_computation | async-start | bytes 4194304 | tf_op jit(solution)/shard_map/all_to_all | solution.py:16
  25.2 0.0 all-gather.3.cloned.1.call-start
  25.3 0.0 copy-done
  25.3 0.1 broadcast_bitcast_fusion
  25.4 0.1 copy.20
  25.5 0.0 copy-done.3
  25.5 0.2 copy.11
  25.6 0.7 broadcast_multiply_fusion
  26.4 0.0 all-gather.3.cloned.1.call-update
  26.4 0.0 all-gather.5.cloned.1.call-start
  26.4 98.9 %all-to-all-done = bf16[32,256,128]{2,1,0:T(8,128)(2,1)S(1)} async-done(((bf16[32,256,128]{2,1,0:T(8,128)(2,1)}), bf16[32,256,128]{2,1,0:T(8,128)(2,1)S(1)}, u32[]{:S(2)}, u32[]{:S(2)}) %all-to-all-start) | async-done | bytes 2097184 | tf_op jit(solution)/shard_map/all_to_all | solution.py:16
  125.3 2.7 copy.12
  128.0 2.8 reshape.19
  130.8 0.0 copy-start.1
  130.8 0.0 all-gather.3.cloned.1.call-done
  130.9 4.2 %fusion.2 = bf16[256,4,128]{0,2,1:T(8,128)(2,1)} fusion(bf16[4096,4,128]{0,2,1:T(8,128)(2,1)} %all-gather.3.cloned.1.call-done, bf16[256,4096,1]{1,0,2:T(8,128)(2,1)S(1)} %reshape.19), kind=kOutput, calls=%fused_computation.4 | convolution fusion | flops 1074003968 | bytes 6553600 | tf_op jit(solution)/shard_map/ik,knj->inj/dot_general | solution.py:18
  135.1 0.0 all-gather.5.cloned.1.call-update
  135.1 0.0 reduce-scatter.2.cloned.1.call-start
  135.2 71.3 %all-gather.5.cloned.1.call-done = bf16[256,4,4096]{0,2,1:T(8,128)(2,1)} async-done(((bf16[256,4,128]{0,2,1:T(8,128)(2,1)}), bf16[256,4,4096]{0,2,1:T(8,128)(2,1)}) %all-gather.5.cloned.1.call-update) | async-done | bytes 8388624 | tf_op jit(solution)/shard_map/all_gather | solution.py:25
  206.5 0.0 copy-done.1
  206.5 8.2 %fusion = bf16[4096,4,128]{0,2,1:T(8,128)(2,1)} fusion(bf16[256,4,128]{0,2,1:T(8,128)(2,1)S(1)} %copy-done.1, bf16[256,4,4096]{0,2,1:T(8,128)(2,1)} %all-gather.5.cloned.1.call-done), kind=kOutput, calls=%fused_computation.1 | convolution fusion | flops 1075838976 | bytes 12845056 | tf_op jit(solution)/shard_map/kni,knj->inj/dot_general | solution.py:27
  214.6 0.0 reduce-scatter.2.cloned.1.call-update
  214.7 0.9 copy-done.4
  215.6 0.2 copy.13
  215.8 0.0 copy-done.2
  215.8 0.9 copy.15
  216.7 88.5 %reduce-scatter.2.cloned.1.call-done = bf16[256,4,128]{0,2,1:T(8,128)(2,1)} async-done(((bf16[4096,4,128]{0,2,1:T(8,128)(2,1)}), bf16[256,4,128]{0,2,1:T(8,128)(2,1)}) %reduce-scatter.2.cloned.1.call-update) | async-done | bytes 262160 | tf_op jit(solution)/shard_map/reduce_scatter | solution.py:26
  305.1 1.0 subtract_convert_fusion
  306.2 0.9 copy.16
  (3 shorter events, 0.0 us)
Async XLA Ops:
  7.2 18.1 %copy-start = (s32[4,32]{1,0:T(4,128)S(1)}, s32[4,32]{1,0:T(4,128)}, u32[]{:S(2)}) copy-start(s32[4,32]{1,0:T(4,128)} %param.7) | copy-start | bytes 1540
  7.2 18.3 %copy-start.3 = (bf16[256,4,128]{2,1,0:T(4,128)(2,1)S(1)}, bf16[256,4,128]{2,1,0:T(4,128)(2,1)}, u32[]{:S(2)}) copy-start(bf16[256,4,128]{2,1,0:T(4,128)(2,1)} %param.5) | copy-start | bytes 786436
  9.9 115.4 %all-to-all-start = ((bf16[32,256,128]{2,1,0:T(8,128)(2,1)}), bf16[32,256,128]{2,1,0:T(8,128)(2,1)S(1)}, u32[]{:S(2)}, u32[]{:S(2)}) async-start(bf16[32,256,128]{2,1,0:T(8,128)(2,1)} %stack.2), calls=%async_computation | async-start | bytes 4194304 | tf_op jit(solution)/shard_map/all_to_all | solution.py:16
  25.2 105.6 %all-gather.3.cloned.1.call-start = ((), (), s32[]{:S(2)}) async-start(), calls=%async_computation.2 | async-start | bytes 4456448 | tf_op jit(solution)/shard_map/all_gather | solution.py:21
  26.4 180.1 %all-gather.5.cloned.1.call-start = ((), (), s32[]{:S(2)}) async-start(), calls=%async_computation.3 | async-start | bytes 8650752 | tf_op jit(solution)/shard_map/all_gather | solution.py:25
  130.8 75.6 %copy-start.1 = (bf16[256,4,128]{0,2,1:T(8,128)(2,1)S(1)}, bf16[256,4,128]{0,2,1:T(8,128)(2,1)}, u32[]{:S(2)}) copy-start(bf16[256,4,128]{0,2,1:T(8,128)(2,1)} %broadcast_multiply_fusion) | copy-start | bytes 786436
  135.1 170.0 %reduce-scatter.2.cloned.1.call-start = ((), (), s32[]{:S(2)}) async-start(), calls=%async_computation.4 | async-start | bytes 4456448 | tf_op jit(solution)/shard_map/reduce_scatter | solution.py:26
  214.6 0.9 copy-start.4
  214.6 1.1 copy-start.2
Sparse Core Ops, SparseCore 0:
  29.6 73.0 all-gather.2
  135.2 71.1 all-gather.4
  214.8 90.3 reduce-scatter.1
